TPU v7x, 256 devices: a whole 4x4x8 slice. The times are simulated.
256 devices in a mesh: tx: 4 (over x_hi, core), ty: 8 (over z), src: 8 (over y, x_lo).
Axes of the slice: x: 4 (x_hi: 2, x_lo: 2; x = x_hi * 2 + x_lo), y: 4, z: 8, core: 2. Of those that a mesh axis runs over, the one named last changes fastest.
Arguments:
- spectrum: bfloat16 [2, 512, 512], P(None, ('tx', 'ty'), 'src'), may hold values from -0.0234375 to 0.0234375
- pupil_mask: int32 [256, 256], replicated, may hold values 0 or 1
- source_shifts: int32 [256, 2], P('src'), may hold values from 0 to 256
- source_weights: int32 [256], P('src'), may hold values from 0 to 8, as said below
Outputs:
- acid_level: float32 [2048, 2048], P(('tx', 'src'), 'ty')
Inputs may be any that keep to these rules, and one draw needn't show every extreme that they name: `source_weights`: the 32 consecutive sources of each group (one index of src) hold at least 4 points with weight above 0; some group has all 32 points on.
All inputs are finite; a program needn't handle non-finite values.
Results may differ from a plain program's by a relative error of at most 0.0017.
Values may be sent and summed in bfloat16 or wider, within the bound.
No kernel may reach another device: no remote copies, remote signals or barrier semaphores. Data moves between devices by JAX's collectives and lax.ppermute only.
A program may use at most 64 MiB of HBM per device.

v0:
```python
import jax
import jax.numpy as jnp
import numpy as np
from jax import lax
from jax.experimental import pallas as pl
from jax.experimental.pallas import tpu as pltpu
from jax.sharding import Mesh
from jax.sharding import PartitionSpec as P

FRAME = 2048
TURN = 2 * FRAME
PASS = 256
MASK_ROWS = 512
SOURCES = 256
ROWS = 64
COLS = 256
SPAN = 72
TABLE_ROWS = 80
BATCH = 4
TOP_WEIGHT = 8
WEIGHT_UNIT = 1 << 18
COLUMN_UNIT = 1 << 9
DIFFUSION = 0.2


def turn_cos_sin(turns):
    shifted = turns + TURN // 8
    quadrant = (shifted >> 10) & 3
    angle = ((shifted & 1023) - TURN // 8).astype(jnp.float32) * (2.0 * jnp.pi / TURN)
    square = angle * angle
    sine = angle * (
        1.0 + square * (-1.0 / 6 + square * (1.0 / 120 + square * (-1.0 / 5040 + square * (1.0 / 362880))))
    )
    cosine = 1.0 + square * (-0.5 + square * (1.0 / 24 + square * (-1.0 / 720 + square * (1.0 / 40320))))
    odd = (quadrant & 1) == 1
    cos_part = jnp.where(odd, sine, cosine)
    sin_part = jnp.where(odd, cosine, sine)
    cos_part = jnp.where((quadrant == 1) | (quadrant == 2), -cos_part, cos_part)
    sin_part = jnp.where(quadrant >= 2, -sin_part, sin_part)
    return cos_part, sin_part


def iota(shape, dim):
    return lax.broadcasted_iota(jnp.int32, shape, dim)


def tables_kernel(place_ref, pupil_ref, row_table, col_table, pupil, phase_cos, phase_sin):
    whole = pupil_ref[...].astype(jnp.float32)
    for part, half in enumerate((whole[:, 0:128], whole[:, 128:256], whole[:, 0:128] - whole[:, 128:256])):
        pupil[part] = half.astype(jnp.bfloat16)

    shape = (TABLE_ROWS, PASS)
    line = iota(shape, 0)
    is_sin = ((line >= 32) & (line < 64)) | (line >= 72)
    pair = jnp.where(line < 64, line & 31, 32 + (line & 1))
    cosine, sine = turn_cos_sin((2 * pair + 1) * (iota(shape, 1) - PASS // 2))
    wave = jnp.where(is_sin, jnp.where((line >= 64) & ((line & 2) == 2), -sine, sine), cosine)
    for weight in range(TOP_WEIGHT + 1):
        row_table[weight] = (weight**0.5 * wave).astype(jnp.bfloat16)

    shape = (PASS, 128)
    frequency = iota(shape, 0) - PASS // 2
    lane = iota(shape, 1)
    cosine, sine = turn_cos_sin((2 * lane + 1) * frequency)
    col_table[:, 0:128] = cosine.astype(jnp.bfloat16)
    col_table[:, 128:256] = sine.astype(jnp.bfloat16)
    cosine, sine = turn_cos_sin((2 * (128 + (lane & 1)) + 1) * frequency)
    col_table[:, 256:384] = cosine.astype(jnp.bfloat16)
    col_table[:, 384:512] = jnp.where((lane & 2) == 0, sine, -sine).astype(jnp.bfloat16)

    row_turns = 2 * place_ref[0] + ROWS - 1
    col_turns = 2 * place_ref[1] + COLS - 1
    shape = (MASK_ROWS, 128)
    row_cos, row_sin = turn_cos_sin(row_turns * iota(shape, 0))
    for tile in range(4):
        col_cos, col_sin = turn_cos_sin(col_turns * (iota((8, 128), 1) + 128 * tile))
        col_cos, col_sin = col_cos[0:1], col_sin[0:1]
        phase_cos[tile] = row_cos * col_cos - row_sin * col_sin
        phase_sin[tile] = row_sin * col_cos + row_cos * col_sin


def image_kernel(
    place_ref, codes_ref, own_ref, other_ref, row_table, col_table, pupil, phase_cos, phase_sin, out_ref,
    spectrum, lhs_even, lhs_odd, plus, minus, edges, order,
):
    row0 = place_ref[0]
    col0 = place_ref[1]
    core = place_ref[2]

    count = jnp.int32(0)
    for s in range(SOURCES):
        code = codes_ref[s // 32, s % 32]
        order[count] = code
        count = count + (code >= WEIGHT_UNIT).astype(jnp.int32)
    for s in range(3 * BATCH):
        order[count + s] = jnp.int32(0)

    low = iota((128, 128), 1) < 64
    for half, ref in ((core, own_ref), (1 - core, other_ref)):
        for xh in range(2):
            base = pl.multiple_of((2 * xh + half) * 128, 128)
            for y in range(4):
                left = ref[xh * 8 + y * 2, 0:128, :].astype(jnp.float32)
                right = ref[xh * 8 + y * 2 + 1, 0:128, :].astype(jnp.float32)
                real = jnp.where(low, left, pltpu.roll(right, 64, 1))
                imag = jnp.where(low, pltpu.roll(left, 64, 1), right)
                cosine = phase_cos[y, pl.ds(base, 128), :]
                sine = phase_sin[y, pl.ds(base, 128), :]
                spectrum[y, pl.ds(base, 128), :] = real * cosine - imag * sine
                spectrum[y, pl.ds(base + MASK_ROWS, 128), :] = real * sine + imag * cosine
    spectrum[4, :, :] = jnp.zeros((2 * MASK_ROWS, 128), jnp.float32)

    plus[...] = jnp.zeros_like(plus)
    minus[...] = jnp.zeros_like(minus)
    edges[...] = jnp.zeros_like(edges)
    sublane_lane = iota((16, 128), 1)
    lane = iota((PASS, 128), 1)
    fold_lane = iota((2 * SPAN, 128), 1)

    def row_transform(index, lhs, members=range(BATCH)):
        for u in members:
            code = order[index * BATCH + u]
            a = code & (COLUMN_UNIT - 1)
            b = (code >> 9) & (COLUMN_UNIT - 1)
            tile = b >> 7
            offset = b & 127
            back = (128 - offset) & 127
            before = (sublane_lane < offset).astype(jnp.bfloat16)
            left, right = [pltpu.roll(pupil[h], offset, 1).reshape(16, 16, 128) for h in range(2)]
            change = before * (left - right)
            masks = [(left - change).reshape(PASS, 128), (right + change).reshape(PASS, 128)]
            turned = []
            for t in range(2):
                window = []
                for part in range(2):
                    rows = pl.ds(a + part * MASK_ROWS, PASS)
                    piece = spectrum[tile + t, rows, :]
                    if t == 0:
                        piece = jnp.where(lane < offset, spectrum[tile + 2, rows, :], piece)
                    window.append(piece.astype(jnp.bfloat16) * masks[t])
                pair = jnp.dot(row_table[code >> 18], jnp.concatenate(window, axis=1), preferred_element_type=jnp.float32)
                rows = []
                for g in range(SPAN // 8):
                    first, second = (8 * (g & 3), 32 + 8 * (g & 3)) if g < 8 else (64, 72)
                    cos_re, sin_re = pair[first : first + 8, 0:128], pair[second : second + 8, 0:128]
                    cos_im, sin_im = pair[first : first + 8, 128:256], pair[second : second + 8, 128:256]
                    rows += [cos_re + sin_im, cos_im - sin_re] if 4 <= g < 8 else [cos_re - sin_im, cos_im + sin_re]
                turned.append(jnp.concatenate(rows, axis=0))
            inside = fold_lane >= offset
            for t in range(2):
                lhs[u * 2 * SPAN : (u + 1) * 2 * SPAN, t * 128 : (t + 1) * 128] = pltpu.roll(
                    jnp.where(inside, turned[t], turned[1 - t]).astype(jnp.bfloat16), back, 1
                )

    def column_transform(index, lhs, members=range(BATCH)):
        span = slice(members[0] * 2 * SPAN, (members[-1] + 1) * 2 * SPAN)
        field = jnp.dot(lhs[span, :], col_table[...], preferred_element_type=jnp.float32)
        for g in range(SPAN // 8):
            here = slice(8 * g, 8 * g + 8)
            sums = [plus[here, :], minus[here, :], edges[here, :]]
            for u in range(len(members)):
                first = u * 2 * SPAN + 16 * g
                real, imag = field[first : first + 8], field[first + 8 : first + 16]
                cos_re, sin_re, cos_im, sin_im = real[:, 0:128], real[:, 128:256], imag[:, 0:128], imag[:, 128:256]
                right_re, right_im = cos_re - sin_im, cos_im + sin_re
                left_re, left_im = cos_re + sin_im, cos_im - sin_re
                edge_re, edge_im = real[:, 256:384] - imag[:, 384:512], imag[:, 256:384] + real[:, 384:512]
                sums[0] = sums[0] + (right_re * right_re + right_im * right_im)
                sums[1] = sums[1] + (left_re * left_re + left_im * left_im)
                sums[2] = sums[2] + (edge_re * edge_re + edge_im * edge_im)
            plus[here, :], minus[here, :], edges[here, :] = sums

    row_transform(0, lhs_even)

    def two_batches(first):
        half = BATCH // 2
        for old, new, step in ((lhs_even, lhs_odd, 0), (lhs_odd, lhs_even, 1)):
            for part in (range(half), range(half, BATCH)):
                column_transform(first + step, old, part)
                row_transform(first + step + 1, new, part)

    def four_batches(index, carry):
        two_batches(4 * index)
        two_batches(4 * index + 2)
        return carry

    batches = jnp.maximum((count + BATCH - 1) // BATCH, 1)
    whole = (batches - 1) // 2
    lax.fori_loop(0, whole // 2, four_batches, 0)

    @pl.when(whole % 2 == 1)
    def odd_pair():
        two_batches(2 * whole - 2)

    column_transform(2 * whole, lhs_even)

    @pl.when(2 * whole + 1 < batches)
    def last_batch():
        row_transform(2 * whole + 1, lhs_odd)
        column_transform(2 * whole + 1, lhs_odd)

    def split(values):
        parts = []
        for _ in range(3):
            parts.append(values.astype(jnp.bfloat16))
            values = values - parts[-1].astype(jnp.float32)
        return parts

    def dot(left, right):
        return jnp.dot(left, right, preferred_element_type=jnp.float32)

    def columns_by(values, choice):
        return sum(dot(part, choice.astype(jnp.bfloat16)) for part in split(values))

    def rows_by(choice, values):
        return sum(dot(choice.astype(jnp.bfloat16), part) for part in split(values))

    source, target = iota((128, 128), 0), iota((128, 128), 1)
    mirror = (source + target == 127).astype(jnp.float32)
    beyond = ((source == target) & (source < 2)) | ((source + target == 129) & (source >= 2) & (source < 4))
    folded = jnp.concatenate(
        [columns_by(minus[...], mirror), plus[...], columns_by(edges[...], beyond.astype(jnp.float32))], axis=1
    )
    target, source = iota((SPAN, SPAN), 0), iota((SPAN, SPAN), 1)
    wanted = jnp.where(
        target < 32, 63 - target, jnp.where(target < 64, target - 32, jnp.where(target < 68, target, 137 - target))
    )
    intensity = rows_by((source == wanted).astype(jnp.float32), folded) * (1.0 / (2 * SOURCES))

    shape = (SPAN, COLS + 128)
    line = iota(shape, 0)
    line = row0 + jnp.where(line < 66, line, line - SPAN)
    pixel = iota(shape, 1)
    pixel = col0 + jnp.where(pixel < COLS + 64, pixel, pixel - (COLS + 128))
    inside = (line >= 0) & (line < FRAME) & (pixel >= 0) & (pixel < FRAME)
    level = jnp.where(inside, 1.0 - jnp.exp(-intensity), 0.0)
    for repeat in range(2):
        beside = (
            pltpu.roll(level, SPAN - 1, 0)
            + pltpu.roll(level, 1, 0)
            + pltpu.roll(level, COLS + 127, 1)
            + pltpu.roll(level, 1, 1)
        )
        level = jnp.where(inside, level + DIFFUSION * (beside - 4.0 * level), 0.0)
    out_ref[...] = level[0:ROWS, 0:COLS]


VMEM_SPEC = pl.BlockSpec(memory_space=pltpu.VMEM)
SMEM_SPEC = pl.BlockSpec(memory_space=pltpu.SMEM)


def make_tables(place, pupil_mask):
    return pl.pallas_call(
        tables_kernel,
        out_shape=(
            jax.ShapeDtypeStruct((TOP_WEIGHT + 1, TABLE_ROWS, PASS), jnp.bfloat16),
            jax.ShapeDtypeStruct((PASS, 512), jnp.bfloat16),
            jax.ShapeDtypeStruct((3, PASS, 128), jnp.bfloat16),
            jax.ShapeDtypeStruct((4, MASK_ROWS, 128), jnp.float32),
            jax.ShapeDtypeStruct((4, MASK_ROWS, 128), jnp.float32),
        ),
        in_specs=[SMEM_SPEC, VMEM_SPEC],
        out_specs=(VMEM_SPEC,) * 5,
        compiler_params=pltpu.CompilerParams(vmem_limit_bytes=16 << 20),
        cost_estimate=pl.CostEstimate(flops=8_000_000, bytes_accessed=3_000_000, transcendentals=0),
    )(place, pupil_mask)


def image_block(place, codes, own, other, tables):
    return pl.pallas_call(
        image_kernel,
        out_shape=jax.ShapeDtypeStruct((ROWS, COLS), jnp.float32),
        in_specs=[SMEM_SPEC, SMEM_SPEC] + [VMEM_SPEC] * 7,
        out_specs=VMEM_SPEC,
        scratch_shapes=[
            pltpu.VMEM((5, 2 * MASK_ROWS, 128), jnp.float32),
            pltpu.VMEM((BATCH * 2 * SPAN, PASS), jnp.bfloat16),
            pltpu.VMEM((BATCH * 2 * SPAN, PASS), jnp.bfloat16),
            pltpu.VMEM((SPAN, 128), jnp.float32),
            pltpu.VMEM((SPAN, 128), jnp.float32),
            pltpu.VMEM((SPAN, 128), jnp.float32),
            pltpu.SMEM((SOURCES + 4 * BATCH,), jnp.int32),
        ],
        compiler_params=pltpu.CompilerParams(vmem_limit_bytes=32 << 20),
    )(place, codes, own, other, *tables)


def gather_blocks(block, axes, count):
    copies = jnp.broadcast_to(block[None], (count,) + block.shape)
    return lax.all_to_all(copies, axes, 0, 0, tiled=True)


def body(spectrum, pupil_mask, source_shifts, source_weights):
    block = jnp.concatenate([spectrum[0], spectrum[1]], axis=1)
    column = gather_blocks(block, ("z",), 8).reshape(128, 128)
    numbers = jnp.concatenate([source_shifts.T, source_weights[None]], axis=0)
    numbers = jnp.pad(numbers, ((0, 5), (0, 96))).astype(jnp.bfloat16)
    own = gather_blocks(jnp.concatenate([column, numbers], axis=0), ("xh", "y", "xl"), 16)
    other = lax.ppermute(own, "core", [(0, 1), (1, 0)])
    listed = own[0:8, 128:136, 0:32].astype(jnp.int32)
    codes = listed[:, 0] + COLUMN_UNIT * listed[:, 1] + WEIGHT_UNIT * listed[:, 2]
    core = lax.axis_index("core")
    tile = 2 * lax.axis_index("xh") + core
    group = 2 * lax.axis_index("y") + lax.axis_index("xl")
    place = jnp.stack([tile * 512 + group * ROWS, lax.axis_index("z") * COLS, core])
    return image_block(place, codes, own, other, make_tables(place, pupil_mask))


def solution(mesh):
    fine = Mesh(np.asarray(mesh.devices).reshape(2, 2, 8, 4, 2), ("xh", "core", "z", "y", "xl"))
    tx, ty, src = ("xh", "core"), "z", ("y", "xl")
    placed = (P(None, (*tx, ty), src), P(), P(src, None), P(src))
    return jax.shard_map(
        body, mesh=fine, in_specs=placed, out_specs=P((*tx, *src), ty), check_vma=False
    )
```

profile of v0, /device:TPU:1, one launch (start us, length us, event | category | flops | bytes accessed | tf_op | source)
XLA Modules:
  0.0 58.9 jit_solution(15180409197897460010)
XLA Ops:
  0.0 0.7 %slice_bitcast_fusion.1 = (bf16[16,64]{1,0:T(8,128)(2,1)S(1)}, bf16[16,64]{1,0:T(8,128)(2,1)S(1)}) fusion(bf16[2,16,64]{2,1,0:T(8,128)(2,1)} %param.4), kind=kLoop, calls=%fused_computation.13 | loop fusion | bytes 8192 | tf_op jit(solution)/shard_map/squeeze | solution.py:294
  0.7 0.1 pad_maximum_fusion.1
  0.8 0.6 %broadcast_in_dim.7 = bf16[8,16,128]{2,1,0:T(8,128)(2,1)} broadcast(bf16[16,128]{1,0:T(8,128)(2,1)S(1)} %pad_maximum_fusion.1), dimensions={1,2} | broadcast | bytes 36864 | tf_op jit(solution)/shard_map/broadcast_in_dim | solution.py:289
  1.4 0.0 copy-start.1
  1.4 9.1 %all-to-all-start = ((bf16[8,16,128]{2,1,0:T(8,128)(2,1)}), bf16[8,16,128]{2,1,0:T(8,128)(2,1)S(1)}, u32[]{:S(2)}, u32[]{:S(2)}) async-start(bf16[8,16,128]{2,1,0:T(8,128)(2,1)} %broadcast_in_dim.7), calls=%async_computation | async-start | bytes 65536 | tf_op jit(solution)/shard_map/all_to_all | solution.py:290
  10.6 0.0 copy-done.1
  10.6 0.0 copy-start.2
  10.6 0.6 %copy-done.2 = s32[32]{0:T(128)S(1)} copy-done((s32[32]{0:T(128)S(1)}, s32[32]{0:T(128)}, u32[]{:S(2)}) %copy-start.2) | copy-done | bytes 152
  11.2 6.2 %all-to-all-done = bf16[8,16,128]{2,1,0:T(8,128)(2,1)S(1)} async-done(((bf16[8,16,128]{2,1,0:T(8,128)(2,1)}), bf16[8,16,128]{2,1,0:T(8,128)(2,1)S(1)}, u32[]{:S(2)}, u32[]{:S(2)}) %all-to-all-start) | async-done | bytes 32800 | tf_op jit(solution)/shard_map/all_to_all | solution.py:290
  17.4 0.9 %broadcast_in_dim.18 = bf16[16,136,128]{2,1,0:T(8,128)(2,1)} broadcast(bf16[136,128]{1,0:T(8,128)(2,1)S(1)} %pad_maximum_fusion), dimensions={1,2} | broadcast | bytes 591872 | tf_op jit(solution)/shard_map/broadcast_in_dim | solution.py:289
  18.3 0.0 copy-start
  18.3 6.9 %all-to-all-start.1 = ((bf16[16,136,128]{2,1,0:T(8,128)(2,1)}), bf16[16,136,128]{2,1,0:T(8,128)(2,1)S(1)}, u32[]{:S(2)}, u32[]{:S(2)}) async-start(bf16[16,136,128]{2,1,0:T(8,128)(2,1)} %broadcast_in_dim.18), calls=%async_computation.1 | async-start | bytes 1114112 | tf_op jit(solution)/shard_map/all_to_all | solution.py:290
  25.2 9.8 %all-to-all-done.1.own_ref = bf16[16,136,128]{2,1,0:T(8,128)(2,1)S(1)} async-done(((bf16[16,136,128]{2,1,0:T(8,128)(2,1)}), bf16[16,136,128]{2,1,0:T(8,128)(2,1)S(1)}, u32[]{:S(2)}, u32[]{:S(2)}) %all-to-all-start.1) | async-done | bytes 557088 | tf_op jit(solution)/shard_map/all_to_all | solution.py:290
  35.1 3.0 %collective-permute-start = (bf16[16,136,128]{2,1,0:T(8,128)(2,1)S(1)}, bf16[16,136,128]{2,1,0:T(8,128)(2,1)S(1)}, u32[]{:S(2)}, u32[]{:S(2)}) collective-permute-start(bf16[16,136,128]{2,1,0:T(8,128)(2,1)S(1)} %all-to-all-done.1.own_ref), channel_id=1, source_target_pairs={{0,64},{64,0},{1,65},{65,1},{2,66},{66,2},{3,67},{67,3},{4,68},{68... | collective-permute-start | bytes 1671176 | tf_op jit(solution)/shard_map/ppermute | solution.py:299
  38.1 0.1 pad_add_fusion.place_ref
  38.2 0.0 copy-done
  38.2 1.7 %shard_map.46 = (bf16[9,80,256]{2,1,0:T(8,128)(2,1)S(1)}, bf16[256,512]{1,0:T(8,128)(2,1)S(1)}, bf16[3,256,128]{2,1,0:T(8,128)(2,1)S(1)}, f32[4,512,128]{2,1,0:T(8,128)S(1)}, f32[4,512,128]{2,1,0:T(8,128)S(1)}) custom-call(s32[3]{0:T(128)S(1)} %pad_add_fusion.place_ref, s32[256,256]{1,0:T(8,128)S(1)} %copy-done), custom_call_target="tpu_custom_call" | custom-call | flops 8000000 | bytes 3000000 | tf_op jit(solution)/shard_map/pallas_call | solution.py:253
  39.9 0.0 collective-permute-done.other_ref
  39.9 19.1 %shard_map.47 = f32[64,256]{1,0:T(8,128)} custom-call(s32[3]{0:T(128)S(1)} %pad_add_fusion.place_ref, s32[8,32]{1,0:T(8,128)S(1)} %bitcast.13, bf16[16,136,128]{2,1,0:T(8,128)(2,1)S(1)} %all-to-all-done.1.own_ref, bf16[16,136,128]{2,1,0:T(8,128)(2,1)S(1)} %collective-permute-done.other_ref, bf16[9,80,256]{2,1,0:T(8,128)(2,1)S(1)} %get-tuple-element.10.row_table, ...), custom_call_target="tpu_custom_call" | custom-call | tf_op jit(solution)/shard_map/pallas_call | solution.py:270
  (6 shorter events, 0.0 us)
Async XLA Ops:
  1.4 9.2 %copy-start.1 = (s32[32,2]{0,1:T(2,128)S(1)}, s32[32,2]{0,1:T(2,128)}, u32[]{:S(2)}) copy-start(s32[32,2]{0,1:T(2,128)} %param.6) | copy-start | bytes 772
  1.4 16.0 %all-to-all-start = ((bf16[8,16,128]{2,1,0:T(8,128)(2,1)}), bf16[8,16,128]{2,1,0:T(8,128)(2,1)S(1)}, u32[]{:S(2)}, u32[]{:S(2)}) async-start(bf16[8,16,128]{2,1,0:T(8,128)(2,1)} %broadcast_in_dim.7), calls=%async_computation | async-start | bytes 65536 | tf_op jit(solution)/shard_map/all_to_all | solution.py:290
  10.6 0.7 %copy-start.2 = (s32[32]{0:T(128)S(1)}, s32[32]{0:T(128)}, u32[]{:S(2)}) copy-start(s32[32]{0:T(128)} %param.7) | copy-start | bytes 388
  18.3 19.9 %copy-start = (s32[256,256]{1,0:T(8,128)S(1)}, s32[256,256]{1,0:T(8,128)}, u32[]{:S(2)}) copy-start(s32[256,256]{1,0:T(8,128)} %pupil_ref.1) | copy-start | bytes 786436
  18.3 16.7 %all-to-all-start.1 = ((bf16[16,136,128]{2,1,0:T(8,128)(2,1)}), bf16[16,136,128]{2,1,0:T(8,128)(2,1)S(1)}, u32[]{:S(2)}, u32[]{:S(2)}) async-start(bf16[16,136,128]{2,1,0:T(8,128)(2,1)} %broadcast_in_dim.18), calls=%async_computation.1 | async-start | bytes 1114112 | tf_op jit(solution)/shard_map/all_to_all | solution.py:290
  35.1 4.8 %collective-permute-start = (bf16[16,136,128]{2,1,0:T(8,128)(2,1)S(1)}, bf16[16,136,128]{2,1,0:T(8,128)(2,1)S(1)}, u32[]{:S(2)}, u32[]{:S(2)}) collective-permute-start(bf16[16,136,128]{2,1,0:T(8,128)(2,1)S(1)} %all-to-all-done.1.own_ref), channel_id=1, source_target_pairs={{0,64},{64,0},{1,65},{65,1},{2,66},{66,2},{3,67},{67,3},{4,68},{68... | collective-permute-start | bytes 1671176 | tf_op jit(solution)/shard_map/ppermute | solution.py:299
where the time goes:
time: 58.2 us; the launch traced here: 58.9 us
  Pallas kernels  20.7 us (36%)
  starting transfers between devices  19.1 us (33%)
  waiting for transfers between devices  16 us (27%)
  local copies, waits for them, and re-layouts  2.84 us (5%)
    pallas_call x1, Pallas kernels, image_block(): pl.pallas_call(image_kernel, out_shape=jax.ShapeDtypeStruct((ROWS, COLS),...  19.1 us
    all_to_all x2, starting transfers between devices, gather_blocks(): return lax.all_to_all(copies, axes, 0, 0, tiled=True)  16 us
    all_to_all x2, waiting for transfers between devices, gather_blocks(): return lax.all_to_all(copies, axes, 0, 0, tiled=True)  16 us
    ppermute x1, starting transfers between devices, body(): other = lax.ppermute(own, 'core', [(0, 1), (1, 0)])  3.04 us
    pallas_call x1, Pallas kernels, make_tables(): pl.pallas_call(tables_kernel, out_shape=(jax.ShapeDtypeStruct((TOP_WEIGHT...  1.66 us
    broadcast_in_dim x2, local copies, waits for them, and re-layouts, gather_blocks(): copies = jnp.broadcast_to(block[None], (count,) + block.shape)  1.49 us
  transfers between devices with their start and end apart: 3, of which 2 were waited for; matrix products, arithmetic and copies ran while one was open for 0% of the time, Pallas kernels for 3%

commit v1 on v0

--- a/solution.py
+++ b/solution.py
@@ -17,6 +17,7 @@
 SPAN = 72
 TABLE_ROWS = 80
 BATCH = 4
+PAIRS = 3
 TOP_WEIGHT = 8
 WEIGHT_UNIT = 1 << 18
 COLUMN_UNIT = 1 << 9
@@ -179,18 +180,20 @@
                 column_transform(first + step, old, part)
                 row_transform(first + step + 1, new, part)
 
-    def four_batches(index, carry):
-        two_batches(4 * index)
-        two_batches(4 * index + 2)
+    def several_pairs(index, carry):
+        for pair in range(PAIRS):
+            two_batches(2 * (PAIRS * index + pair))
+        return carry
+
+    def one_pair(index, carry):
+        two_batches(2 * index)
         return carry
 
     batches = jnp.maximum((count + BATCH - 1) // BATCH, 1)
     whole = (batches - 1) // 2
-    lax.fori_loop(0, whole // 2, four_batches, 0)
-
-    @pl.when(whole % 2 == 1)
-    def odd_pair():
-        two_batches(2 * whole - 2)
+    turns = whole // PAIRS
+    lax.fori_loop(0, turns, several_pairs, 0)
+    lax.fori_loop(PAIRS * turns, whole, one_pair, 0)
 
     column_transform(2 * whole, lhs_even)
 

time: 58.2 us -> 56.6 us (0.973)
  Pallas kernels: 20.7 us -> 18.6 us
    pallas_call x1, Pallas kernels: 19.1 us -> 17 us  [image_block(): pl.pallas_call(image_kernel, out_shape=jax.ShapeDtypeStruct((ROWS, COLS),...]
where the time goes in v1:
time: 56.6 us; the launch traced here: 56.9 us
  starting transfers between devices  19.1 us (34%)
  Pallas kernels  18.6 us (33%)
  waiting for transfers between devices  16 us (28%)
  local copies, waits for them, and re-layouts  2.84 us (5%)
    pallas_call x1, Pallas kernels, image_block(): pl.pallas_call(image_kernel, out_shape=jax.ShapeDtypeStruct((ROWS, COLS),...  17 us
    all_to_all x2, starting transfers between devices, gather_blocks(): return lax.all_to_all(copies, axes, 0, 0, tiled=True)  16 us
    all_to_all x2, waiting for transfers between devices, gather_blocks(): return lax.all_to_all(copies, axes, 0, 0, tiled=True)  16 us
    ppermute x1, starting transfers between devices, body(): other = lax.ppermute(own, 'core', [(0, 1), (1, 0)])  3.04 us
    pallas_call x1, Pallas kernels, make_tables(): pl.pallas_call(tables_kernel, out_shape=(jax.ShapeDtypeStruct((TOP_WEIGHT...  1.66 us
    broadcast_in_dim x2, local copies, waits for them, and re-layouts, gather_blocks(): copies = jnp.broadcast_to(block[None], (count,) + block.shape)  1.49 us
  transfers between devices with their start and end apart: 3, of which 2 were waited for; matrix products, arithmetic and copies ran while one was open for 0% of the time, Pallas kernels for 3%

profile of v1, /device:TPU:1, one launch (start us, length us, event | category | flops | bytes accessed | tf_op | source)
XLA Modules:
  0.0 56.9 jit_solution(10838421818806661792)
XLA Ops:
  0.0 0.7 %slice_bitcast_fusion.1 = (bf16[16,64]{1,0:T(8,128)(2,1)S(1)}, bf16[16,64]{1,0:T(8,128)(2,1)S(1)}) fusion(bf16[2,16,64]{2,1,0:T(8,128)(2,1)} %param.4), kind=kLoop, calls=%fused_computation.13 | loop fusion | bytes 8192 | tf_op jit(solution)/shard_map/squeeze | solution.py:297
  0.7 0.1 pad_maximum_fusion.1
  0.8 0.6 %broadcast_in_dim.7 = bf16[8,16,128]{2,1,0:T(8,128)(2,1)} broadcast(bf16[16,128]{1,0:T(8,128)(2,1)S(1)} %pad_maximum_fusion.1), dimensions={1,2} | broadcast | bytes 36864 | tf_op jit(solution)/shard_map/broadcast_in_dim | solution.py:292
  1.4 0.0 copy-start.1
  1.4 9.1 %all-to-all-start = ((bf16[8,16,128]{2,1,0:T(8,128)(2,1)}), bf16[8,16,128]{2,1,0:T(8,128)(2,1)S(1)}, u32[]{:S(2)}, u32[]{:S(2)}) async-start(bf16[8,16,128]{2,1,0:T(8,128)(2,1)} %broadcast_in_dim.7), calls=%async_computation | async-start | bytes 65536 | tf_op jit(solution)/shard_map/all_to_all | solution.py:293
  10.6 0.0 copy-done.1
  10.6 0.0 copy-start.2
  10.6 0.6 %copy-done.2 = s32[32]{0:T(128)S(1)} copy-done((s32[32]{0:T(128)S(1)}, s32[32]{0:T(128)}, u32[]{:S(2)}) %copy-start.2) | copy-done | bytes 152
  11.2 6.2 %all-to-all-done = bf16[8,16,128]{2,1,0:T(8,128)(2,1)S(1)} async-done(((bf16[8,16,128]{2,1,0:T(8,128)(2,1)}), bf16[8,16,128]{2,1,0:T(8,128)(2,1)S(1)}, u32[]{:S(2)}, u32[]{:S(2)}) %all-to-all-start) | async-done | bytes 32800 | tf_op jit(solution)/shard_map/all_to_all | solution.py:293
  17.4 0.9 %broadcast_in_dim.18 = bf16[16,136,128]{2,1,0:T(8,128)(2,1)} broadcast(bf16[136,128]{1,0:T(8,128)(2,1)S(1)} %pad_maximum_fusion), dimensions={1,2} | broadcast | bytes 591872 | tf_op jit(solution)/shard_map/broadcast_in_dim | solution.py:292
  18.3 0.0 copy-start
  18.3 6.9 %all-to-all-start.1 = ((bf16[16,136,128]{2,1,0:T(8,128)(2,1)}), bf16[16,136,128]{2,1,0:T(8,128)(2,1)S(1)}, u32[]{:S(2)}, u32[]{:S(2)}) async-start(bf16[16,136,128]{2,1,0:T(8,128)(2,1)} %broadcast_in_dim.18), calls=%async_computation.1 | async-start | bytes 1114112 | tf_op jit(solution)/shard_map/all_to_all | solution.py:293
  25.2 9.8 %all-to-all-done.1.own_ref = bf16[16,136,128]{2,1,0:T(8,128)(2,1)S(1)} async-done(((bf16[16,136,128]{2,1,0:T(8,128)(2,1)}), bf16[16,136,128]{2,1,0:T(8,128)(2,1)S(1)}, u32[]{:S(2)}, u32[]{:S(2)}) %all-to-all-start.1) | async-done | bytes 557088 | tf_op jit(solution)/shard_map/all_to_all | solution.py:293
  35.1 3.0 %collective-permute-start = (bf16[16,136,128]{2,1,0:T(8,128)(2,1)S(1)}, bf16[16,136,128]{2,1,0:T(8,128)(2,1)S(1)}, u32[]{:S(2)}, u32[]{:S(2)}) collective-permute-start(bf16[16,136,128]{2,1,0:T(8,128)(2,1)S(1)} %all-to-all-done.1.own_ref), channel_id=1, source_target_pairs={{0,64},{64,0},{1,65},{65,1},{2,66},{66,2},{3,67},{67,3},{4,68},{68... | collective-permute-start | bytes 1671176 | tf_op jit(solution)/shard_map/ppermute | solution.py:302
  38.1 0.1 pad_add_fusion.place_ref
  38.2 0.0 copy-done
  38.2 1.7 %shard_map.46 = (bf16[9,80,256]{2,1,0:T(8,128)(2,1)S(1)}, bf16[256,512]{1,0:T(8,128)(2,1)S(1)}, bf16[3,256,128]{2,1,0:T(8,128)(2,1)S(1)}, f32[4,512,128]{2,1,0:T(8,128)S(1)}, f32[4,512,128]{2,1,0:T(8,128)S(1)}) custom-call(s32[3]{0:T(128)S(1)} %pad_add_fusion.place_ref, s32[256,256]{1,0:T(8,128)S(1)} %copy-done), custom_call_target="tpu_custom_call" | custom-call | flops 8000000 | bytes 3000000 | tf_op jit(solution)/shard_map/pallas_call | solution.py:256
  39.9 0.0 collective-permute-done.other_ref
  39.9 17.0 %shard_map.47 = f32[64,256]{1,0:T(8,128)} custom-call(s32[3]{0:T(128)S(1)} %pad_add_fusion.place_ref, s32[8,32]{1,0:T(8,128)S(1)} %bitcast.13, bf16[16,136,128]{2,1,0:T(8,128)(2,1)S(1)} %all-to-all-done.1.own_ref, bf16[16,136,128]{2,1,0:T(8,128)(2,1)S(1)} %collective-permute-done.other_ref, bf16[9,80,256]{2,1,0:T(8,128)(2,1)S(1)} %get-tuple-element.10.row_table, ...), custom_call_target="tpu_custom_call" | custom-call | tf_op jit(solution)/shard_map/pallas_call | solution.py:273
  (6 shorter events, 0.0 us)
Async XLA Ops:
  1.4 9.2 %copy-start.1 = (s32[32,2]{0,1:T(2,128)S(1)}, s32[32,2]{0,1:T(2,128)}, u32[]{:S(2)}) copy-start(s32[32,2]{0,1:T(2,128)} %param.6) | copy-start | bytes 772
  1.4 16.0 %all-to-all-start = ((bf16[8,16,128]{2,1,0:T(8,128)(2,1)}), bf16[8,16,128]{2,1,0:T(8,128)(2,1)S(1)}, u32[]{:S(2)}, u32[]{:S(2)}) async-start(bf16[8,16,128]{2,1,0:T(8,128)(2,1)} %broadcast_in_dim.7), calls=%async_computation | async-start | bytes 65536 | tf_op jit(solution)/shard_map/all_to_all | solution.py:293
  10.6 0.7 %copy-start.2 = (s32[32]{0:T(128)S(1)}, s32[32]{0:T(128)}, u32[]{:S(2)}) copy-start(s32[32]{0:T(128)} %param.7) | copy-start | bytes 388
  18.3 19.9 %copy-start = (s32[256,256]{1,0:T(8,128)S(1)}, s32[256,256]{1,0:T(8,128)}, u32[]{:S(2)}) copy-start(s32[256,256]{1,0:T(8,128)} %pupil_ref.1) | copy-start | bytes 786436
  18.3 16.7 %all-to-all-start.1 = ((bf16[16,136,128]{2,1,0:T(8,128)(2,1)}), bf16[16,136,128]{2,1,0:T(8,128)(2,1)S(1)}, u32[]{:S(2)}, u32[]{:S(2)}) async-start(bf16[16,136,128]{2,1,0:T(8,128)(2,1)} %broadcast_in_dim.18), calls=%async_computation.1 | async-start | bytes 1114112 | tf_op jit(solution)/shard_map/all_to_all | solution.py:293
  35.1 4.8 %collective-permute-start = (bf16[16,136,128]{2,1,0:T(8,128)(2,1)S(1)}, bf16[16,136,128]{2,1,0:T(8,128)(2,1)S(1)}, u32[]{:S(2)}, u32[]{:S(2)}) collective-permute-start(bf16[16,136,128]{2,1,0:T(8,128)(2,1)S(1)} %all-to-all-done.1.own_ref), channel_id=1, source_target_pairs={{0,64},{64,0},{1,65},{65,1},{2,66},{66,2},{3,67},{67,3},{4,68},{68... | collective-permute-start | bytes 1671176 | tf_op jit(solution)/shard_map/ppermute | solution.py:302
